TPU v7x, 32 devices: a whole 2x2x4 slice. The times are simulated.
32 devices in a mesh: row: 8 (over z, core), col: 4 (over y, x).
Axes of the slice: x: 2, y: 2, z: 4, core: 2. Of those that a mesh axis runs over, the one named last changes fastest.
Arguments:
- sire_index: int32 [1024], P('row'), may hold values from 0 to 4095
- dam_index: int32 [1024], P('row'), may hold values from -1 to 4095, as said below
- relatives: float32 [4096, 4, 2048], P('row', None, 'col'), may hold values from 0 to 1
- factor_blocks: float32 [6, 2048, 2048], P(None, 'row', 'col'), may hold values from -0.125 to 0.125
- inverses: float32 [4, 2048, 2048], P(None, 'col'), as said below
Outputs:
- relationship: float32 [4, 2048, 1024], P(None, 'col', 'row')
- border: float32 [4, 2048, 1024], P(None, 'col', 'row')
Inputs may be any that keep to these rules, and one draw needn't show every extreme that they name: `dam_index`: -1 marks an unknown dam; every other value is a row of relatives. `inverses`: lower triangular, with diagonal entries of 0.6 to 1.4.
All inputs are finite; a program needn't handle non-finite values.
Results may differ from a plain program's by a relative error of at most 0.0001.
Values sent between devices are 32-bit elements; how exact they have to be, the bound alone decides.
A program may use at most 128 MiB of HBM per device.

v0:
```python
import jax
import jax.numpy as jnp
from jax import lax
from jax.sharding import PartitionSpec as P


def product(left, right):
    return jnp.dot(left, right, precision=lax.Precision.HIGHEST, preferred_element_type=jnp.float32)


def fetch_rows(stacked):
    return lax.all_gather(stacked, "row", axis=0, tiled=True)


def per_device(sire_index, dam_index, relatives, factor_blocks, inverses):
    calf_dev = sire_index.shape[0]
    old_dev, blocks, block_cols = relatives.shape
    flat_rows = relatives.reshape(old_dev, blocks * block_cols)
    all_sires, all_dams = (
        lax.all_gather(sire_index, "row", axis=0, tiled=True),
        lax.all_gather(dam_index, "row", axis=0, tiled=True),
    )
    owned = lax.axis_index("row") * old_dev + lax.iota(jnp.int32, old_dev)
    picks = 0.5 * (
        (all_sires[:, None] == owned[None, :]).astype(jnp.float32)
        + (all_dams[:, None] == owned[None, :]).astype(jnp.float32)
    )
    mine = lax.psum_scatter(product(picks, flat_rows), "row", scatter_dimension=0, tiled=True)
    relation = mine.T
    relationship = relation.reshape(blocks, block_cols, calf_dev)
    solved = []
    for target in range(blocks):
        remain = relationship[target]
        if target > 0:
            needed = jnp.stack(
                [factor_blocks[target * (target - 1) // 2 + source] for source in range(target)],
                axis=1,
            )
            whole_rows = fetch_rows(needed).reshape(-1, target * block_cols)
            earlier = jnp.concatenate(solved, axis=0)

            def earlier_terms(start, count, whole_rows=whole_rows, earlier=earlier):
                return product(whole_rows, earlier)

            remain = remain - lax.psum_scatter(
                earlier_terms(jnp.int32(0), block_cols * lax.axis_size("col")),
                "col",
                scatter_dimension=0,
                tiled=True,
            )
        own_inverse = inverses[target]
        solved.append(product(own_inverse, lax.all_gather(remain, "col", axis=0, tiled=True)))
    return (relationship, jnp.stack(solved))


def solution(mesh):
    return jax.shard_map(
        per_device,
        mesh=mesh,
        in_specs=(
            P("row"),
            P("row"),
            P("row", None, "col"),
            P(None, "row", "col"),
            P(None, "col", None),
        ),
        out_specs=(P(None, "col", "row"), P(None, "col", "row")),
        check_vma=False,
    )
```

profile of v0, /device:TPU:0, one launch (start us, length us, event | category | flops | bytes accessed | tf_op | source)
XLA Modules:
  0.0 627.8 jit_solution(4835952748387480247)
XLA Ops:
  7.2 6.1 copy.33
  13.4 13.4 %all-gather.1 = s32[8,1,128]{2,1,0:T(1,128)S(1)} all-gather(s32[1,1,128]{2,1,0:T(1,128)S(1)} %bitcast.82), channel_id=1, replica_groups=mesh['row'=8,'col'=4] {'row'}, dimensions={0}, use_global_device_ids=true | all-gather | bytes 4608 | tf_op jit(solution)/shard_map/all_gather | solution.py:20
  26.8 8.7 %all-gather.2 = s32[8,1,128]{2,1,0:T(1,128)S(1)} all-gather(s32[1,1,128]{2,1,0:T(1,128)S(1)} %bitcast.83), channel_id=1, replica_groups=mesh['row'=8,'col'=4] {'row'}, dimensions={0}, use_global_device_ids=true | all-gather | bytes 4608 | tf_op jit(solution)/shard_map/all_gather | solution.py:21
  35.5 17.8 %fusion.17 = f32[1024,2048]{1,0:T(8,128)} fusion(f32[512,2048]{1,0:T(8,128)} %bitcast.68, s32[512]{0:T(512)S(1)} %iota_add_fusion, s32[1024]{0:T(1024)S(1)} %bitcast.81, s32[1024]{0:T(1024)S(1)} %bitcast.80), kind=kOutput, calls=%fused_computation.15 | convolution fusion | flops 12888047616 | bytes 12593152 | tf_op jit(solution)/shard_map/dot_general | solution.py:8
  53.5 89.0 %reduce-scatter.5.cloned.1.call-done = f32[128,2048]{1,0:T(8,128)} async-done(((f32[1024,2048]{1,0:T(8,128)}), f32[128,2048]{1,0:T(8,128)}) %reduce-scatter.5.cloned.1.call-update) | async-done | bytes 1048592 | tf_op jit(solution)/shard_map/reduce_scatter | solution.py:28
  144.2 3.2 fusion.44
  147.6 21.7 %all-gather.11.cloned.1.call-done = f32[2048,128]{0,1:T(8,128)} async-done(((f32[512,128]{0,1:T(8,128)}), f32[2048,128]{0,1:T(8,128)}) %all-gather.11.cloned.1.call-update) | async-done | bytes 1048592 | tf_op jit(solution)/shard_map/all_gather | solution.py:52
  169.3 6.9 %fusion.8 = f32[128,512]{1,0:T(8,128)S(1)} fusion(f32[2048,128]{0,1:T(8,128)} %all-gather.11.cloned.1.call-done, f32[4,512,2048]{2,1,0:T(8,128)} %param.9), kind=kOutput, calls=%fused_computation.8 | convolution fusion | flops 1610612736 | bytes 5505024 | tf_op jit(solution)/shard_map/dot_general | solution.py:8
  176.1 42.2 %all-gather.23.cloned.1.call-done = f32[1,2048,512]{2,1,0:T(8,128)} async-done(((f32[1,256,512]{2,1,0:T(8,128)}), f32[1,2048,512]{2,1,0:T(8,128)}) %all-gather.23.cloned.1.call-update) | async-done | bytes 4194320 | tf_op jit(solution)/shard_map/all_gather | solution.py:12
  218.3 7.5 %fusion.14 = f32[2048,128]{0,1:T(8,128)} fusion(f32[128,512]{1,0:T(8,128)S(1)} %fusion.8, f32[1,2048,512]{2,1,0:T(8,128)} %all-gather.23.cloned.1.call-done), kind=kOutput, calls=%fused_computation.14 | convolution fusion | flops 1610612736 | bytes 5505024 | tf_op jit(solution)/shard_map/dot_general | solution.py:8
  225.9 26.8 %reduce-scatter.7.cloned.1.call-done = f32[512,128]{0,1:T(8,128)} async-done(((f32[2048,128]{0,1:T(8,128)}), f32[512,128]{0,1:T(8,128)}) %reduce-scatter.7.cloned.1.call-update) | async-done | bytes 262160 | tf_op jit(solution)/shard_map/reduce_scatter | solution.py:45
  261.1 20.0 %all-gather.13.cloned.1.call-done = f32[2048,128]{0,1:T(8,128)} async-done(((f32[512,128]{0,1:T(8,128)}), f32[2048,128]{0,1:T(8,128)}) %all-gather.13.cloned.1.call-update) | async-done | bytes 1048592 | tf_op jit(solution)/shard_map/all_gather | solution.py:52
  281.1 6.9 %fusion.4 = f32[128,512]{1,0:T(8,128)S(1)} fusion(f32[2048,128]{0,1:T(8,128)} %all-gather.13.cloned.1.call-done, f32[4,512,2048]{2,1,0:T(8,128)} %param.9), kind=kOutput, calls=%fused_computation.4 | convolution fusion | flops 1610612736 | bytes 5505024 | tf_op jit(solution)/shard_map/dot_general | solution.py:8
  287.9 77.2 %all-gather.15.cloned.1.call-done = f32[2048,2,512]{0,2,1:T(8,128)} async-done(((f32[256,2,512]{0,2,1:T(8,128)}), f32[2048,2,512]{0,2,1:T(8,128)}) %all-gather.15.cloned.1.call-update) | async-done | bytes 8388624 | tf_op jit(solution)/shard_map/all_gather | solution.py:12
  365.2 8.1 %fusion.37 = f32[2048,128]{0,1:T(8,128)} fusion(f32[2048,1024]{0,1:T(8,128)} %bitcast.58, f32[512,128]{0,1:T(8,128)S(1)} %bitcast.69, f32[512,128]{0,1:T(8,128)S(1)} %bitcast.59), kind=kOutput, calls=%fused_computation.36 | convolution fusion | flops 3221356544 | bytes 9961472 | tf_op jit(solution)/shard_map/dot_general | solution.py:8
  373.3 26.5 %reduce-scatter.9.cloned.1.call-done = f32[512,128]{0,1:T(8,128)} async-done(((f32[2048,128]{0,1:T(8,128)}), f32[512,128]{0,1:T(8,128)}) %reduce-scatter.9.cloned.1.call-update) | async-done | bytes 262160 | tf_op jit(solution)/shard_map/reduce_scatter | solution.py:45
  403.0 2.3 pad_maximum_fusion
  405.7 23.1 %all-gather.17.cloned.1.call-done = f32[2048,128]{0,1:T(8,128)} async-done(((f32[512,128]{0,1:T(8,128)}), f32[2048,128]{0,1:T(8,128)}) %all-gather.17.cloned.1.call-update) | async-done | bytes 1048592 | tf_op jit(solution)/shard_map/all_gather | solution.py:52
  428.8 6.9 %fusion.2 = f32[128,512]{1,0:T(8,128)S(1)} fusion(f32[2048,128]{0,1:T(8,128)} %all-gather.17.cloned.1.call-done, f32[4,512,2048]{2,1,0:T(8,128)} %param.9), kind=kOutput, calls=%fused_computation.2 | convolution fusion | flops 1610612736 | bytes 5505024 | tf_op jit(solution)/shard_map/dot_general | solution.py:8
  435.7 111.5 %all-gather.19.cloned.1.call-done = f32[2048,3,512]{0,2,1:T(8,128)} async-done(((f32[256,3,512]{0,2,1:T(8,128)}), f32[2048,3,512]{0,2,1:T(8,128)}) %all-gather.19.cloned.1.call-update) | async-done | bytes 12582928 | tf_op jit(solution)/shard_map/all_gather | solution.py:12
  547.2 10.6 %fusion.31 = f32[2048,128]{0,1:T(8,128)} fusion(f32[2048,1536]{0,1:T(8,128)} %bitcast.57, f32[512,128]{0,1:T(8,128)S(1)} %bitcast.72, f32[512,128]{0,1:T(8,128)S(1)} %bitcast.70, f32[512,128]{0,1:T(8,128)S(1)} %bitcast.60), kind=kOutput, calls=%fused_computation.30 | convolution fusion | flops 4832231424 | bytes 14417920 | tf_op jit(solution)/shard_map/dot_general | solution.py:8
  557.9 26.2 %reduce-scatter.11.cloned.1.call-done = f32[512,128]{0,1:T(8,128)} async-done(((f32[2048,128]{0,1:T(8,128)}), f32[512,128]{0,1:T(8,128)}) %reduce-scatter.11.cloned.1.call-update) | async-done | bytes 262160 | tf_op jit(solution)/shard_map/reduce_scatter | solution.py:45
  587.1 26.0 %all-gather.21.cloned.1.call-done = f32[2048,128]{0,1:T(8,128)} async-done(((f32[512,128]{0,1:T(8,128)}), f32[2048,128]{0,1:T(8,128)}) %all-gather.21.cloned.1.call-update) | async-done | bytes 1048592 | tf_op jit(solution)/shard_map/all_gather | solution.py:52
  613.0 6.9 %fusion.24 = f32[1,512,128]{1,2,0:T(8,128)S(1)} fusion(f32[2048,128]{0,1:T(8,128)} %all-gather.21.cloned.1.call-done, f32[4,512,2048]{2,1,0:T(8,128)} %param.9), kind=kOutput, calls=%fused_computation.23 | convolution fusion | flops 1610612736 | bytes 5505024 | tf_op jit(solution)/shard_map/dot_general | solution.py:8
  (42 shorter events, 18.4 us)
Async XLA Ops:
  7.2 135.3 %reduce-scatter.5.cloned.1.call-start = ((), (), s32[]{:S(2)}) async-start(), calls=%async_computation.4 | async-start | bytes 9437184 | tf_op jit(solution)/shard_map/reduce_scatter | solution.py:28
  7.2 6.2 copy-start.1
  7.2 19.6 %copy-start.2 = (s32[128]{0:T(128)S(1)}, s32[128]{0:T(128)}, u32[]{:S(2)}) copy-start(s32[128]{0:T(128)} %param.6) | copy-start | bytes 1540
  53.4 115.8 %all-gather.11.cloned.1.call-start = ((), (), s32[]{:S(2)}) async-start(), calls=%async_computation.5 | async-start | bytes 1310720 | tf_op jit(solution)/shard_map/all_gather | solution.py:52
  144.1 74.2 %all-gather.23.cloned.1.call-start = ((), (), s32[]{:S(2)}) async-start(), calls=%async_computation.14 | async-start | bytes 4718592 | tf_op jit(solution)/shard_map/all_gather | solution.py:12
  147.4 105.3 %reduce-scatter.7.cloned.1.call-start = ((), (), s32[]{:S(2)}) async-start(), calls=%async_computation.6 | async-start | bytes 1310720 | tf_op jit(solution)/shard_map/reduce_scatter | solution.py:45
  176.1 76.6 %copy-start = (f32[128,2048]{1,0:T(8,128)S(1)}, f32[128,2048]{1,0:T(8,128)}, u32[]{:S(2)}) copy-start(f32[128,2048]{1,0:T(8,128)} %reduce-scatter.5.cloned.1.call-done) | copy-start | bytes 3145732
  225.8 55.3 %all-gather.13.cloned.1.call-start = ((), (), s32[]{:S(2)}) async-start(), calls=%async_computation.7 | async-start | bytes 1310720 | tf_op jit(solution)/shard_map/all_gather | solution.py:52
  254.4 110.8 %all-gather.15.cloned.1.call-start = ((), (), s32[]{:S(2)}) async-start(), calls=%async_computation.8 | async-start | bytes 9437184 | tf_op jit(solution)/shard_map/all_gather | solution.py:12
  260.8 139.0 %reduce-scatter.9.cloned.1.call-start = ((), (), s32[]{:S(2)}) async-start(), calls=%async_computation.9 | async-start | bytes 1310720 | tf_op jit(solution)/shard_map/reduce_scatter | solution.py:45
  373.3 55.5 %all-gather.17.cloned.1.call-start = ((), (), s32[]{:S(2)}) async-start(), calls=%async_computation.10 | async-start | bytes 1310720 | tf_op jit(solution)/shard_map/all_gather | solution.py:52
  401.6 145.6 %all-gather.19.cloned.1.call-start = ((), (), s32[]{:S(2)}) async-start(), calls=%async_computation.11 | async-start | bytes 14155776 | tf_op jit(solution)/shard_map/all_gather | solution.py:12
  405.4 178.7 %reduce-scatter.11.cloned.1.call-start = ((), (), s32[]{:S(2)}) async-start(), calls=%async_computation.12 | async-start | bytes 1310720 | tf_op jit(solution)/shard_map/reduce_scatter | solution.py:45
  557.8 55.2 %all-gather.21.cloned.1.call-start = ((), (), s32[]{:S(2)}) async-start(), calls=%async_computation.13 | async-start | bytes 1310720 | tf_op jit(solution)/shard_map/all_gather | solution.py:52
Sparse Core Ops, SparseCore 0:
  53.5 88.8 reduce-scatter.4
  144.3 24.9 all-gather.10
  171.4 46.8 all-gather.22
  225.9 26.7 reduce-scatter.6
  254.5 26.4 all-gather.12
  283.1 82.0 all-gather.14
  373.4 26.4 reduce-scatter.8
  402.3 26.4 all-gather.16
  430.4 116.6 all-gather.18
  557.9 26.0 reduce-scatter.10
  586.5 26.4 all-gather.20
where the time goes:
time: 628 us
  waiting for transfers between devices  490 us (78%)
  matrix products  71.4 us (11%)
  blocking collectives  22.2 us (4%)
  local copies, waits for them, and re-layouts  19.1 us (3%)
  between operations  14 us (2%)
  other arithmetic  9.71 us (2%)
    all_gather x3, waiting for transfers between devices, fetch_rows(): return lax.all_gather(stacked, 'row', axis=0, tiled=True)  231 us
    all_gather x4, waiting for transfers between devices, per_device(): lax.all_gather(remain, 'col', axis=0, tiled=True)  90.7 us
    reduce_scatter x1, waiting for transfers between devices, per_device(): lax.psum_scatter(product(picks, flat_rows), 'row', scatter_dimension=0, t...  89 us
    reduce_scatter x3, waiting for transfers between devices, per_device(): lax.psum_scatter(earlier_terms(jnp.int32(0), block_cols * lax.axis_size('...  79.6 us
    dot_general x8, matrix products, product(): jnp.dot(left, right, precision=lax.Precision.HIGHEST, preferred_element_t...  71.4 us
    unnamed x14, local copies, waits for them, and re-layouts  14.2 us
    all_gather x1, blocking collectives, per_device(): lax.all_gather(sire_index, 'row', axis=0, tiled=True)  13.4 us
  transfers between devices with their start and end apart: 11, of which 11 were waited for; matrix products, arithmetic and copies ran while one was open for 6% of the time, Pallas kernels for 0%

commit v1 on v0

--- a/solution.py
+++ b/solution.py
@@ -2,6 +2,19 @@
 import jax.numpy as jnp
 from jax import lax
 from jax.sharding import PartitionSpec as P
+
+
+def collect(value, axis, dim):
+    size, place, rows = (lax.axis_size(axis), lax.axis_index(axis), value.shape[dim])
+    forward = [(i, (i + 1) % size) for i in range(size)]
+    out = jnp.zeros((*value.shape[:dim], size * rows, *value.shape[dim + 1 :]), value.dtype)
+    block = value
+    for lap in range(size):
+        owner = (place - lap) % size
+        out = lax.dynamic_update_slice_in_dim(out, block, owner * rows, axis=dim)
+        if lap < size - 1:
+            block = lax.ppermute(block, axis, forward)
+    return out
 
 
 def product(left, right):
@@ -9,7 +22,7 @@
 
 
 def fetch_rows(stacked):
-    return lax.all_gather(stacked, "row", axis=0, tiled=True)
+    return collect(stacked, "row", 0)
 
 
 def per_device(sire_index, dam_index, relatives, factor_blocks, inverses):

time: 628 us -> 507 us (0.81); the launches traced: 628 us -> 498 us
  waiting for transfers between devices: 490 us -> 298 us
  local copies, waits for them, and re-layouts: 19.1 us -> 80.9 us
    ppermute x0 -> x21, waiting for transfers between devices: none -> 233 us  [collect(): block = lax.ppermute(block, axis, forward)]
    all_gather x3 -> x0, waiting for transfers between devices: 231 us -> none  [fetch_rows(): return lax.all_gather(stacked, 'row', axis=0, tiled=True)]
    reduce_scatter x1, waiting for transfers between devices: 89 us -> 0.01 us  [per_device(): lax.psum_scatter(product(picks, flat_rows), 'row', scatter_dimension=0, t...]
    all_gather x4, waiting for transfers between devices: 90.7 us -> 33.5 us  [per_device(): lax.all_gather(remain, 'col', axis=0, tiled=True)]
    reduce_scatter x3, waiting for transfers between devices: 79.6 us -> 31.5 us  [per_device(): lax.psum_scatter(earlier_terms(jnp.int32(0), block_cols * lax.axis_size('...]
    dynamic_update_slice x0 -> x22, local copies, waits for them, and re-layouts: none -> 44.8 us  [collect(): out = lax.dynamic_update_slice_in_dim(out, block, owner * rows, axis=dim)]
    broadcast_in_dim x0 -> x2, local copies, waits for them, and re-layouts: none -> 10.5 us  [collect(): jnp.zeros((*value.shape[:dim], size * rows, *value.shape[dim + 1:]), valu...]
    unnamed x14 -> x28, local copies, waits for them, and re-layouts: 14.2 us -> 19.7 us
  transfers between devices with their start and end apart: 11 -> 29, of which waited for: 11 -> 18; matrix products, arithmetic and copies ran while one was open for 6% -> 22% of each run, Pallas kernels for 0% -> 0%
where the time goes in v1:
time: 507 us; the launch traced here: 498 us
  waiting for transfers between devices  298 us (59%)
  local copies, waits for them, and re-layouts  80.9 us (16%)
  matrix products  70.1 us (14%)
  blocking collectives  22.2 us (4%)
  between operations  14.6 us (3%)
  other arithmetic  8.38 us (2%)
    ppermute x21, waiting for transfers between devices, collect(): block = lax.ppermute(block, axis, forward)  233 us
    dot_general x8, matrix products, product(): jnp.dot(left, right, precision=lax.Precision.HIGHEST, preferred_element_t...  70.1 us
    dynamic_update_slice x22, local copies, waits for them, and re-layouts, collect(): out = lax.dynamic_update_slice_in_dim(out, block, owner * rows, axis=dim)  44.8 us
    all_gather x4, waiting for transfers between devices, per_device(): lax.all_gather(remain, 'col', axis=0, tiled=True)  33.5 us
    reduce_scatter x3, waiting for transfers between devices, per_device(): lax.psum_scatter(earlier_terms(jnp.int32(0), block_cols * lax.axis_size('...  31.5 us
    unnamed x28, local copies, waits for them, and re-layouts  19.7 us
    all_gather x1, blocking collectives, per_device(): lax.all_gather(sire_index, 'row', axis=0, tiled=True)  13.5 us
    broadcast_in_dim x2, local copies, waits for them, and re-layouts, collect(): jnp.zeros((*value.shape[:dim], size * rows, *value.shape[dim + 1:]), valu...  10.5 us
  transfers between devices with their start and end apart: 29, of which 18 were waited for; matrix products, arithmetic and copies ran while one was open for 22% of the time, Pallas kernels for 0%

profile of v1, /device:TPU:0, one launch (start us, length us, event | category | flops | bytes accessed | tf_op | source)
XLA Modules:
  0.0 497.7 jit_solution(8394106655780898703)
XLA Ops:
  11.4 13.5 %all-gather = s32[8,1,128]{2,1,0:T(1,128)S(1)} all-gather(s32[1,1,128]{2,1,0:T(1,128)S(1)} %bitcast.92), channel_id=1, replica_groups=mesh['row'=8,'col'=4] {'row'}, dimensions={0}, use_global_device_ids=true | all-gather | bytes 4608 | tf_op jit(solution)/shard_map/all_gather | solution.py:33
  24.9 8.7 %all-gather.1 = s32[8,1,128]{2,1,0:T(1,128)S(1)} all-gather(s32[1,1,128]{2,1,0:T(1,128)S(1)} %bitcast.93), channel_id=1, replica_groups=mesh['row'=8,'col'=4] {'row'}, dimensions={0}, use_global_device_ids=true | all-gather | bytes 4608 | tf_op jit(solution)/shard_map/all_gather | solution.py:34
  33.6 16.3 %fusion.12 = f32[1024,2048]{1,0:T(8,128)} fusion(f32[512,2048]{1,0:T(8,128)S(1)} %bitcast.78, s32[512]{0:T(512)S(1)} %iota_add_fusion, s32[1024]{0:T(1024)S(1)} %bitcast.91, s32[1024]{0:T(1024)S(1)} %bitcast.90), kind=kOutput, calls=%fused_computation.12 | convolution fusion | flops 12888047616 | bytes 12593152 | tf_op jit(solution)/shard_map/dot_general | solution.py:21
  65.0 8.8 %collective-permute-done = f32[256,1,512]{2,0,1:T(8,128)} collective-permute-done((f32[256,1,512]{2,0,1:T(8,128)}, f32[256,1,512]{2,0,1:T(8,128)}, u32[]{:S(2)}, u32[]{:S(2)}) %collective-permute-start) | collective-permute-done | bytes 524320 | tf_op jit(solution)/shard_map/ppermute | solution.py:16
  73.9 50.5 %collective-permute-done.1 = f32[256,1,512]{2,0,1:T(8,128)S(1)} collective-permute-done((f32[256,1,512]{2,0,1:T(8,128)}, f32[256,1,512]{2,0,1:T(8,128)S(1)}, u32[]{:S(2)}, u32[]{:S(2)}) %collective-permute-start.1) | collective-permute-done | bytes 524320 | tf_op jit(solution)/shard_map/ppermute | solution.py:16
  125.7 20.5 %collective-permute-done.2 = f32[256,1,512]{2,0,1:T(8,128)} collective-permute-done((f32[256,1,512]{2,0,1:T(8,128)S(1)}, f32[256,1,512]{2,0,1:T(8,128)}, u32[]{:S(2)}, u32[]{:S(2)}) %collective-permute-start.2) | collective-permute-done | bytes 524320 | tf_op jit(solution)/shard_map/ppermute | solution.py:16
  161.0 21.2 %collective-permute-done.3 = f32[256,1,512]{2,0,1:T(8,128)} collective-permute-done((f32[256,1,512]{2,0,1:T(8,128)}, f32[256,1,512]{2,0,1:T(8,128)}, u32[]{:S(2)}, u32[]{:S(2)}) %collective-permute-start.3) | collective-permute-done | bytes 524320 | tf_op jit(solution)/shard_map/ppermute | solution.py:16
  185.5 19.1 %collective-permute-done.4 = f32[256,1,512]{2,0,1:T(8,128)} collective-permute-done((f32[256,1,512]{2,0,1:T(8,128)}, f32[256,1,512]{2,0,1:T(8,128)}, u32[]{:S(2)}, u32[]{:S(2)}) %collective-permute-start.4) | collective-permute-done | bytes 524320 | tf_op jit(solution)/shard_map/ppermute | solution.py:16
  212.1 9.3 %collective-permute-done.5 = f32[256,1,512]{2,0,1:T(8,128)S(1)} collective-permute-done((f32[256,1,512]{2,0,1:T(8,128)}, f32[256,1,512]{2,0,1:T(8,128)S(1)}, u32[]{:S(2)}, u32[]{:S(2)}) %collective-permute-start.5) | collective-permute-done | bytes 524320 | tf_op jit(solution)/shard_map/ppermute | solution.py:16
  226.0 17.9 %collective-permute-done.6 = f32[256,1,512]{2,0,1:T(8,128)S(1)} collective-permute-done((f32[256,1,512]{2,0,1:T(8,128)S(1)}, f32[256,1,512]{2,0,1:T(8,128)S(1)}, u32[]{:S(2)}, u32[]{:S(2)}) %collective-permute-start.6) | collective-permute-done | bytes 524320 | tf_op jit(solution)/shard_map/ppermute | solution.py:16
  244.7 6.9 %fusion.6 = f32[128,512]{1,0:T(8,128)S(1)} fusion(f32[2048,128]{0,1:T(8,128)} %all-gather.7.cloned.1.call-done, f32[4,512,2048]{2,1,0:T(8,128)} %param.9), kind=kOutput, calls=%fused_computation.6 | convolution fusion | flops 1610612736 | bytes 5505024 | tf_op jit(solution)/shard_map/dot_general | solution.py:21
  251.6 7.7 %fusion.39 = f32[2048,128]{0,1:T(8,128)} fusion(f32[2048,512]{1,0:T(8,128)} %bitcast_dynamic-update-slice_fusion, f32[128,512]{1,0:T(8,128)S(1)} %fusion.6), kind=kOutput, calls=%fused_computation.69 | convolution fusion | flops 1610612736 | bytes 5505024 | tf_op jit(solution)/shard_map/dot_general | solution.py:21
  259.5 32.9 %collective-permute-done.11 = f32[256,2,512]{0,2,1:T(8,128)} collective-permute-done((f32[256,2,512]{0,2,1:T(8,128)}, f32[256,2,512]{0,2,1:T(8,128)}, u32[]{:S(2)}, u32[]{:S(2)}) %collective-permute-start.11) | collective-permute-done | bytes 1048608 | tf_op jit(solution)/shard_map/ppermute | solution.py:16
  294.2 14.5 %collective-permute-done.12 = f32[256,2,512]{0,2,1:T(8,128)} collective-permute-done((f32[256,2,512]{0,2,1:T(8,128)}, f32[256,2,512]{0,2,1:T(8,128)}, u32[]{:S(2)}, u32[]{:S(2)}) %collective-permute-start.12) | collective-permute-done | bytes 1048608 | tf_op jit(solution)/shard_map/ppermute | solution.py:16
  328.1 8.6 %collective-permute-done.13 = f32[256,2,512]{0,2,1:T(8,128)S(1)} collective-permute-done((f32[256,2,512]{0,2,1:T(8,128)}, f32[256,2,512]{0,2,1:T(8,128)S(1)}, u32[]{:S(2)}, u32[]{:S(2)}) %collective-permute-start.13) | collective-permute-done | bytes 1048608 | tf_op jit(solution)/shard_map/ppermute | solution.py:16
  337.8 6.9 %fusion.4 = f32[128,512]{1,0:T(8,128)S(1)} fusion(f32[2048,128]{0,1:T(8,128)} %all-gather.9.cloned.1.call-done, f32[4,512,2048]{2,1,0:T(8,128)} %param.9), kind=kOutput, calls=%fused_computation.4 | convolution fusion | flops 1610612736 | bytes 5505024 | tf_op jit(solution)/shard_map/dot_general | solution.py:21
  344.7 8.1 %fusion.32 = f32[2048,128]{0,1:T(8,128)} fusion(f32[2048,1024]{0,1:T(8,128)} %bitcast.23, f32[512,128]{0,1:T(8,128)S(1)} %bitcast.79, f32[512,128]{0,1:T(8,128)S(1)} %bitcast.69), kind=kOutput, calls=%fused_computation.33 | convolution fusion | flops 3221356544 | bytes 9961472 | tf_op jit(solution)/shard_map/dot_general | solution.py:21
  353.6 22.0 %collective-permute-done.19 = f32[256,3,512]{0,2,1:T(8,128)} collective-permute-done((f32[256,3,512]{0,2,1:T(8,128)}, f32[256,3,512]{0,2,1:T(8,128)}, u32[]{:S(2)}, u32[]{:S(2)}) %collective-permute-start.19) | collective-permute-done | bytes 1572896 | tf_op jit(solution)/shard_map/ppermute | solution.py:16
  400.3 7.6 %all-gather.11.cloned.1.call-done = f32[2048,128]{0,1:T(8,128)} async-done(((f32[512,128]{0,1:T(8,128)}), f32[2048,128]{0,1:T(8,128)}) %all-gather.11.cloned.1.call-update) | async-done | bytes 1048592 | tf_op jit(solution)/shard_map/all_gather | solution.py:65
  407.9 6.9 %fusion.2 = f32[128,512]{1,0:T(8,128)S(1)} fusion(f32[2048,128]{0,1:T(8,128)} %all-gather.11.cloned.1.call-done, f32[4,512,2048]{2,1,0:T(8,128)} %param.9), kind=kOutput, calls=%fused_computation.2 | convolution fusion | flops 1610612736 | bytes 5505024 | tf_op jit(solution)/shard_map/dot_general | solution.py:21
  414.7 10.6 %fusion.26 = f32[2048,128]{0,1:T(8,128)} fusion(f32[2048,1536]{0,1:T(8,128)} %bitcast.30, f32[512,128]{0,1:T(8,128)S(1)} %bitcast.82, f32[512,128]{0,1:T(8,128)S(1)} %bitcast.80, f32[512,128]{0,1:T(8,128)S(1)} %bitcast.70), kind=kOutput, calls=%fused_computation.27 | convolution fusion | flops 4832231424 | bytes 14417920 | tf_op jit(solution)/shard_map/dot_general | solution.py:21
  425.4 28.0 %reduce-scatter.11.cloned.1.call-done = f32[512,128]{0,1:T(8,128)} async-done(((f32[2048,128]{0,1:T(8,128)}), f32[512,128]{0,1:T(8,128)}) %reduce-scatter.11.cloned.1.call-update) | async-done | bytes 262160 | tf_op jit(solution)/shard_map/reduce_scatter | solution.py:58
  456.5 25.9 %all-gather.13.cloned.1.call-done = f32[2048,128]{0,1:T(8,128)} async-done(((f32[512,128]{0,1:T(8,128)}), f32[2048,128]{0,1:T(8,128)}) %all-gather.13.cloned.1.call-update) | async-done | bytes 1048592 | tf_op jit(solution)/shard_map/all_gather | solution.py:65
  482.4 6.9 %fusion.19 = f32[1,512,128]{1,2,0:T(8,128)S(1)} fusion(f32[2048,128]{0,1:T(8,128)} %all-gather.13.cloned.1.call-done, f32[4,512,2048]{2,1,0:T(8,128)} %param.9), kind=kOutput, calls=%fused_computation.20 | convolution fusion | flops 1610612736 | bytes 5505024 | tf_op jit(solution)/shard_map/dot_general | solution.py:21
  (114 shorter events, 104.1 us)
Async XLA Ops:
  7.2 197.5 %reduce-scatter.5.cloned.1.call-start = ((), (), s32[]{:S(2)}) async-start(), calls=%async_computation.4 | async-start | bytes 9437184 | tf_op jit(solution)/shard_map/reduce_scatter | solution.py:41
  49.9 194.8 %all-gather.7.cloned.1.call-start = ((), (), s32[]{:S(2)}) async-start(), calls=%async_computation.5 | async-start | bytes 1310720 | tf_op jit(solution)/shard_map/all_gather | solution.py:65
  63.5 60.8 %collective-permute-start.7 = (f32[256,2,512]{0,2,1:T(8,128)S(1)}, f32[256,2,512]{0,2,1:T(8,128)}, u32[]{:S(2)}, u32[]{:S(2)}) collective-permute-start(f32[256,2,512]{0,2,1:T(8,128)S(1)} %get-tuple-element.16), channel_id=1, source_target_pairs={{0,4},{4,8},{8,12},{12,16},{16,20},{20,24},{24,28},{28,0},{1,5},{5... | collective-permute-start | bytes 3145736 | tf_op jit(solution)/shard_map/ppermute | solution.py:16
  73.9 50.5 %collective-permute-start.1 = (f32[256,1,512]{2,0,1:T(8,128)}, f32[256,1,512]{2,0,1:T(8,128)S(1)}, u32[]{:S(2)}, u32[]{:S(2)}) collective-permute-start(f32[256,1,512]{2,0,1:T(8,128)} %collective-permute-done), channel_id=1, source_target_pairs={{0,4},{4,8},{8,12},{12,16},{16,20},{20,24},{24,28},{28,0},{1,5},{5... | collective-permute-start | bytes 1572872 | tf_op jit(solution)/shard_map/ppermute | solution.py:16
  125.2 60.4 %collective-permute-start.8 = (f32[256,2,512]{0,2,1:T(8,128)}, f32[256,2,512]{0,2,1:T(8,128)}, u32[]{:S(2)}, u32[]{:S(2)}) collective-permute-start(f32[256,2,512]{0,2,1:T(8,128)} %collective-permute-done.7), channel_id=1, source_target_pairs={{0,4},{4,8},{8,12},{12,16},{16,20},{20,24},{24,28},{28,0},{1,5},{5... | collective-permute-start | bytes 3145736 | tf_op jit(solution)/shard_map/ppermute | solution.py:16
  146.2 36.0 %collective-permute-start.3 = (f32[256,1,512]{2,0,1:T(8,128)}, f32[256,1,512]{2,0,1:T(8,128)}, u32[]{:S(2)}, u32[]{:S(2)}) collective-permute-start(f32[256,1,512]{2,0,1:T(8,128)} %collective-permute-done.2), channel_id=1, source_target_pairs={{0,4},{4,8},{8,12},{12,16},{16,20},{20,24},{24,28},{28,0},{1,5},{5... | collective-permute-start | bytes 1572872 | tf_op jit(solution)/shard_map/ppermute | solution.py:16
  161.0 51.1 %collective-permute-start.14 = (f32[256,3,512]{0,2,1:T(8,128)}, f32[256,3,512]{0,2,1:T(8,128)}, u32[]{:S(2)}, u32[]{:S(2)}) collective-permute-start(f32[256,3,512]{0,2,1:T(8,128)} %get-tuple-element.14), channel_id=1, source_target_pairs={{0,4},{4,8},{8,12},{12,16},{16,20},{20,24},{24,28},{28,0},{1,5},{5... | collective-permute-start | bytes 4718600 | tf_op jit(solution)/shard_map/ppermute | solution.py:16
  182.2 22.5 %collective-permute-start.4 = (f32[256,1,512]{2,0,1:T(8,128)}, f32[256,1,512]{2,0,1:T(8,128)}, u32[]{:S(2)}, u32[]{:S(2)}) collective-permute-start(f32[256,1,512]{2,0,1:T(8,128)} %collective-permute-done.3), channel_id=1, source_target_pairs={{0,4},{4,8},{8,12},{12,16},{16,20},{20,24},{24,28},{28,0},{1,5},{5... | collective-permute-start | bytes 1572872 | tf_op jit(solution)/shard_map/ppermute | solution.py:16
  185.5 39.6 %collective-permute-start.9 = (f32[256,2,512]{0,2,1:T(8,128)}, f32[256,2,512]{0,2,1:T(8,128)}, u32[]{:S(2)}, u32[]{:S(2)}) collective-permute-start(f32[256,2,512]{0,2,1:T(8,128)} %collective-permute-done.8), channel_id=1, source_target_pairs={{0,4},{4,8},{8,12},{12,16},{16,20},{20,24},{24,28},{28,0},{1,5},{5... | collective-permute-start | bytes 3145736 | tf_op jit(solution)/shard_map/ppermute | solution.py:16
  206.3 86.1 %reduce-scatter.7.cloned.1.call-start = ((), (), s32[]{:S(2)}) async-start(), calls=%async_computation.6 | async-start | bytes 1310720 | tf_op jit(solution)/shard_map/reduce_scatter | solution.py:58
  212.1 47.2 %collective-permute-start.15 = (f32[256,3,512]{0,2,1:T(8,128)}, f32[256,3,512]{0,2,1:T(8,128)S(1)}, u32[]{:S(2)}, u32[]{:S(2)}) collective-permute-start(f32[256,3,512]{0,2,1:T(8,128)} %collective-permute-done.14), channel_id=1, source_target_pairs={{0,4},{4,8},{8,12},{12,16},{16,20},{20,24},{24,28},{28,0},{1,5},{5... | collective-permute-start | bytes 4718600 | tf_op jit(solution)/shard_map/ppermute | solution.py:16
  221.4 22.5 %collective-permute-start.6 = (f32[256,1,512]{2,0,1:T(8,128)S(1)}, f32[256,1,512]{2,0,1:T(8,128)S(1)}, u32[]{:S(2)}, u32[]{:S(2)}) collective-permute-start(f32[256,1,512]{2,0,1:T(8,128)S(1)} %collective-permute-done.5), channel_id=1, source_target_pairs={{0,4},{4,8},{8,12},{12,16},{16,20},{20,24},{24,28},{28,0},{1,5},{5... | collective-permute-start | bytes 1572872 | tf_op jit(solution)/shard_map/ppermute | solution.py:16
  225.1 34.2 %collective-permute-start.10 = (f32[256,2,512]{0,2,1:T(8,128)}, f32[256,2,512]{0,2,1:T(8,128)}, u32[]{:S(2)}, u32[]{:S(2)}) collective-permute-start(f32[256,2,512]{0,2,1:T(8,128)} %collective-permute-done.9), channel_id=1, source_target_pairs={{0,4},{4,8},{8,12},{12,16},{16,20},{20,24},{24,28},{28,0},{1,5},{5... | collective-permute-start | bytes 3145736 | tf_op jit(solution)/shard_map/ppermute | solution.py:16
  259.3 78.5 %all-gather.9.cloned.1.call-start = ((), (), s32[]{:S(2)}) async-start(), calls=%async_computation.7 | async-start | bytes 1310720 | tf_op jit(solution)/shard_map/all_gather | solution.py:65
  259.3 33.0 %collective-permute-start.16 = (f32[256,3,512]{0,2,1:T(8,128)S(1)}, f32[256,3,512]{0,2,1:T(8,128)}, u32[]{:S(2)}, u32[]{:S(2)}) collective-permute-start(f32[256,3,512]{0,2,1:T(8,128)S(1)} %collective-permute-done.15), channel_id=1, source_target_pairs={{0,4},{4,8},{8,12},{12,16},{16,20},{20,24},{24,28},{28,0},{1,5},{5... | collective-permute-start | bytes 4718600 | tf_op jit(solution)/shard_map/ppermute | solution.py:16
  259.4 33.0 %collective-permute-start.11 = (f32[256,2,512]{0,2,1:T(8,128)}, f32[256,2,512]{0,2,1:T(8,128)}, u32[]{:S(2)}, u32[]{:S(2)}) collective-permute-start(f32[256,2,512]{0,2,1:T(8,128)} %collective-permute-done.10), channel_id=1, source_target_pairs={{0,4},{4,8},{8,12},{12,16},{16,20},{20,24},{24,28},{28,0},{1,5},{5... | collective-permute-start | bytes 3145736 | tf_op jit(solution)/shard_map/ppermute | solution.py:16
  292.4 33.2 %collective-permute-start.17 = (f32[256,3,512]{0,2,1:T(8,128)}, f32[256,3,512]{0,2,1:T(8,128)}, u32[]{:S(2)}, u32[]{:S(2)}) collective-permute-start(f32[256,3,512]{0,2,1:T(8,128)} %collective-permute-done.16), channel_id=1, source_target_pairs={{0,4},{4,8},{8,12},{12,16},{16,20},{20,24},{24,28},{28,0},{1,5},{5... | collective-permute-start | bytes 4718600 | tf_op jit(solution)/shard_map/ppermute | solution.py:16
  294.1 85.0 %reduce-scatter.9.cloned.1.call-start = ((), (), s32[]{:S(2)}) async-start(), calls=%async_computation.8 | async-start | bytes 1310720 | tf_op jit(solution)/shard_map/reduce_scatter | solution.py:58
  308.7 28.0 %collective-permute-start.13 = (f32[256,2,512]{0,2,1:T(8,128)}, f32[256,2,512]{0,2,1:T(8,128)S(1)}, u32[]{:S(2)}, u32[]{:S(2)}) collective-permute-start(f32[256,2,512]{0,2,1:T(8,128)} %collective-permute-done.12), channel_id=1, source_target_pairs={{0,4},{4,8},{8,12},{12,16},{16,20},{20,24},{24,28},{28,0},{1,5},{5... | collective-permute-start | bytes 3145736 | tf_op jit(solution)/shard_map/ppermute | solution.py:16
  325.5 28.1 %collective-permute-start.18 = (f32[256,3,512]{0,2,1:T(8,128)}, f32[256,3,512]{0,2,1:T(8,128)}, u32[]{:S(2)}, u32[]{:S(2)}) collective-permute-start(f32[256,3,512]{0,2,1:T(8,128)} %collective-permute-done.17), channel_id=1, source_target_pairs={{0,4},{4,8},{8,12},{12,16},{16,20},{20,24},{24,28},{28,0},{1,5},{5... | collective-permute-start | bytes 4718600 | tf_op jit(solution)/shard_map/ppermute | solution.py:16
  352.8 55.1 %all-gather.11.cloned.1.call-start = ((), (), s32[]{:S(2)}) async-start(), calls=%async_computation.9 | async-start | bytes 1310720 | tf_op jit(solution)/shard_map/all_gather | solution.py:65
  353.6 22.0 %collective-permute-start.19 = (f32[256,3,512]{0,2,1:T(8,128)}, f32[256,3,512]{0,2,1:T(8,128)}, u32[]{:S(2)}, u32[]{:S(2)}) collective-permute-start(f32[256,3,512]{0,2,1:T(8,128)} %collective-permute-done.18), channel_id=1, source_target_pairs={{0,4},{4,8},{8,12},{12,16},{16,20},{20,24},{24,28},{28,0},{1,5},{5... | collective-permute-start | bytes 4718600 | tf_op jit(solution)/shard_map/ppermute | solution.py:16
  380.8 72.7 %reduce-scatter.11.cloned.1.call-start = ((), (), s32[]{:S(2)}) async-start(), calls=%async_computation.10 | async-start | bytes 1310720 | tf_op jit(solution)/shard_map/reduce_scatter | solution.py:58
  425.4 57.0 %all-gather.13.cloned.1.call-start = ((), (), s32[]{:S(2)}) async-start(), calls=%async_computation.11 | async-start | bytes 1310720 | tf_op jit(solution)/shard_map/all_gather | solution.py:65
  (15 other events, 189.9 us)
Sparse Core Ops, SparseCore 0:
  50.0 125.9 reduce-scatter.4
  206.5 27.7 all-gather.6
  259.4 26.1 reduce-scatter.6
  294.2 28.0 all-gather.8
  352.9 26.1 reduce-scatter.8
  381.4 26.4 all-gather.10
  425.5 27.9 reduce-scatter.10
  455.9 26.4 all-gather.12
